TPU v7x, 256 devices: a whole 4x4x8 slice. The times are simulated.
256 devices in a mesh: dp: 64 (over z, y, core), tensor: 4 (over x).
Axes of the slice: x: 4, y: 4, z: 8, core: 2. Of those that a mesh axis runs over, the one named last changes fastest.
Arguments:
- gradient: float32 [48, 1024, 1024], P(None, 'dp', 'tensor'), may hold values from -90 to 90
- second_moment: float32 [48, 1024, 1024], P(None, 'dp', 'tensor'), may hold values from 0.1 to 1
- owner_table: int32 [48], replicated, may hold values from 0 to 63, as said below
- slot_table: int32 [48], replicated, may hold values from 0 to 1, as said below
- left_stat: float32 [64, 2, 1024, 1024], P('dp', None, 'tensor'), may hold values from -1 to 4
- right_stat: float32 [64, 2, 1024, 1024], P('dp', None, 'tensor'), may hold values from -1 to 4
- left_root: bfloat16 [64, 2, 1024, 1024], P('dp', None, 'tensor'), may hold values from -1 to 4
- right_root: bfloat16 [64, 2, 1024, 1024], P('dp', None, 'tensor'), may hold values from -1 to 4
Outputs:
- update: bfloat16 [48, 1024, 1024], P(None, 'dp', 'tensor')
- new_second: float32 [48, 1024, 1024], P(None, 'dp', 'tensor')
- left_new: float32 [64, 2, 1024, 1024], P('dp', None, 'tensor')
- right_new: float32 [64, 2, 1024, 1024], P('dp', None, 'tensor')
Inputs may be any that keep to these rules, and one draw needn't show every extreme that they name: The pairs (owner_table[b], slot_table[b]) are distinct; each owner holds at most 2 blocks, and some owner holds exactly 2; owners 0 and 63 each hold at least one block. `slot_table`: paired with owner_table as stated there.
All inputs are finite; a program needn't handle non-finite values.
Results may differ from a plain program's by a relative error of at most 0.0064.
Values may be sent and summed in bfloat16 or wider, within the bound.
A program may use at most 64 MiB of HBM per device.

v0:
```python
import jax
import jax.numpy as jnp
from jax import lax
from jax.sharding import PartitionSpec as P


def per_device(
    gradient, second_moment, owner_table, slot_table, left_stat, right_stat, left_root, right_root
):
    blocks, shard_rows, shard_cols = gradient.shape
    owner_count = lax.axis_size("dp")
    slot_count = left_stat.shape[1]
    stripe = left_stat.shape[2]
    block_order = left_stat.shape[3]
    owner_index = lax.axis_index("dp")
    tensor_index = lax.axis_index("tensor")
    flat_index = owner_table * slot_count + slot_table
    new_second = 0.99 * second_moment + 0.01 * gradient * gradient
    adam = gradient / (jnp.sqrt(new_second) + 1e-08)
    adam_part = jnp.sum(adam * adam, axis=(1, 2))
    grad_low = gradient.astype(jnp.bfloat16)
    gathered = lax.all_gather(grad_low, "tensor", axis=2, tiled=True)
    buffer = (
        jnp.zeros((owner_count * slot_count, shard_rows, block_order), jnp.bfloat16)
        .at[flat_index]
        .set(gathered)
    )
    whole = lax.all_to_all(buffer, "dp", split_axis=0, concat_axis=1, tiled=True)
    row_part = lax.dynamic_slice_in_dim(whole, tensor_index * stripe, stripe, 1)
    col_part = lax.dynamic_slice_in_dim(whole, tensor_index * stripe, stripe, 2)
    left_term = jnp.einsum("sik,sjk->sij", row_part, whole, preferred_element_type=jnp.float32)
    right_term = jnp.einsum("ski,skj->sij", col_part, whole, preferred_element_type=jnp.float32)
    left_new = 0.5 * left_stat + 0.5 / block_order * left_term[None]
    right_new = 0.5 * right_stat + 0.5 / block_order * right_term[None]
    mixed = jnp.einsum(
        "sik,skj->sij", left_root[0], whole, preferred_element_type=jnp.float32
    ).astype(jnp.bfloat16)
    product = jnp.einsum(
        "sik,skj->sij",
        mixed,
        lax.all_gather(right_root[0], "tensor", axis=1, tiled=True),
        preferred_element_type=jnp.float32,
    )
    precond = product.astype(jnp.bfloat16)
    precond_wide = precond.astype(jnp.float32)
    root_slot = jnp.sum(precond_wide * precond_wide, axis=(1, 2))
    returned = lax.all_to_all(
        lax.all_to_all(precond, "tensor", split_axis=2, concat_axis=1, tiled=True),
        "dp",
        split_axis=1,
        concat_axis=0,
        tiled=True,
    )
    returned_blocks = returned[flat_index]
    slot_match = slot_table[:, None] == jnp.arange(slot_count, dtype=jnp.int32)[None, :]
    looked_up = jnp.sum(jnp.where(slot_match, root_slot[None, :], 0.0), axis=1)
    root_part = jnp.where(owner_table == owner_index, looked_up, 0.0)
    adam_total, root_total = lax.psum((adam_part, root_part), ("dp", "tensor"))
    graft_scale = jnp.sqrt(adam_total / (root_total + 1e-06))
    update = (graft_scale[:, None, None] * returned_blocks.astype(jnp.float32)).astype(jnp.bfloat16)
    return (update, new_second, left_new, right_new)


def solution(mesh):
    placed = (
        P(None, "dp", "tensor"),
        P(None, "dp", "tensor"),
        P(),
        P(),
        P("dp", None, "tensor", None),
        P("dp", None, "tensor", None),
        P("dp", None, "tensor", None),
        P("dp", None, "tensor", None),
    )
    return jax.shard_map(
        per_device,
        mesh=mesh,
        in_specs=placed,
        out_specs=(
            P(None, "dp", "tensor"),
            P(None, "dp", "tensor"),
            P("dp", None, "tensor", None),
            P("dp", None, "tensor", None),
        ),
        check_vma=False,
    )
```

profile of v0, /device:TPU:1, one launch (start us, length us, event | category | flops | bytes accessed | tf_op | source)
XLA Modules:
  0.0 296.8 jit_solution(7836436570167904347)
XLA Ops:
  7.2 0.0 copy-start
  7.2 0.0 copy-start.4
  7.2 0.0 copy-start.5
  7.2 0.0 all-gather.4.cloned.1.call-start
  7.2 3.2 %multiply_reduce_fusion.1 = (f32[48]{0:T(128)S(1)}, f32[48,16,256]{2,1,0:T(8,128)}, bf16[48,16,256]{2,1,0:T(8,128)(2,1)}) fusion(f32[48,16,256]{2,1,0:T(8,128)} %param.8, f32[48,16,256]{2,1,0:T(8,128)} %param.9), kind=kLoop, calls=%fused_computation.15 | loop fusion | flops 1769424 | bytes 2752704 | tf_op jit(solution)/shard_map/reduce_sum | solution.py:20
  10.4 0.0 all-gather.4.cloned.1.call-update
  10.5 0.0 copy-done.4
  10.5 0.0 copy-done.5
  10.5 34.7 %all-gather.4.cloned.1.call-done = bf16[48,16,1024]{2,1,0:T(8,128)(2,1)} async-done(((bf16[48,16,256]{2,1,0:T(8,128)(2,1)}), bf16[48,16,1024]{2,1,0:T(8,128)(2,1)}) %all-gather.4.cloned.1.call-update) | async-done | bytes 1572880 | tf_op jit(solution)/shard_map/all_gather | solution.py:22
  45.2 0.0 copy-start.3
  45.2 2.5 broadcast_in_dim.29
  47.7 0.0 copy-done.3
  47.7 6.6 %scatter_fusion = bf16[128,16,1024]{2,1,0:T(8,128)(2,1)} fusion(bf16[128,16,1024]{2,1,0:T(8,128)(2,1)} %broadcast_in_dim.29, s32[48]{0:T(128)S(1)} %compare_select_fusion, bf16[48,16,1024]{2,1,0:T(8,128)(2,1)S(1)} %copy-done.3), kind=kCustom, calls=%fused_computation.1 | custom fusion | bytes 4718784 | tf_op jit(solution)/shard_map/scatter | solution.py:26
  54.3 12.2 %all-to-all-start = ((bf16[128,16,1024]{2,1,0:T(8,128)(2,1)}), bf16[128,16,1024]{2,1,0:T(8,128)(2,1)}, u32[]{:S(2)}, u32[]{:S(2)}) async-start(bf16[128,16,1024]{2,1,0:T(8,128)(2,1)} %scatter_fusion), calls=%async_computation | async-start | bytes 8388608 | tf_op jit(solution)/shard_map/all_to_all | solution.py:28
  66.5 0.0 all-gather.6.cloned.1.call-start
  66.6 0.7 all-gather.6.cloned.1.call-update
  67.3 94.0 %all-to-all-done = bf16[128,16,1024]{2,1,0:T(8,128)(2,1)} async-done(((bf16[128,16,1024]{2,1,0:T(8,128)(2,1)}), bf16[128,16,1024]{2,1,0:T(8,128)(2,1)}, u32[]{:S(2)}, u32[]{:S(2)}) %all-to-all-start) | async-done | bytes 4194336 | tf_op jit(solution)/shard_map/all_to_all | solution.py:28
  161.2 5.0 %copy.34 = bf16[2,64,16,1024]{3,2,1,0:T(8,128)(2,1)} copy(bf16[2,64,16,1024]{3,2,0,1:T(8,128)(2,1)} %bitcast.1) | data formatting | bytes 8388608 | tf_op jit(solution)/shard_map/all_to_all | solution.py:28
  166.2 0.0 all-gather.6.cloned.1.call-done
  166.2 0.0 copy-done
  166.2 6.1 %multiply_reduce_fusion = (f32[2]{0:T(128)S(1)}, bf16[2,256,1024]{2,1,0:T(8,128)(2,1)S(1)}) fusion(bf16[1,2,1024,1024]{3,2,1,0:T(8,128)(2,1)} %all-gather.6.cloned.1.call-done, bf16[2,1024,1024]{2,1,0:T(8,128)(2,1)} %bitcast.33, bf16[1,2,256,1024]{3,2,1,0:T(8,128)(2,1)S(1)} %copy-done), kind=kOutput, calls=%fused_computation.6 | convolution fusion | flops 2150105088 | bytes 10485768 | tf_op jit(solution)/shard_map/sik,skj->sij/dot_general | solution.py:38
  172.4 0.9 copy.37
  173.3 16.3 %all_to_all.54 = bf16[2,256,1024]{1,0,2:T(2,128)(2,1)S(1)} all-to-all(bf16[2,256,1024]{1,0,2:T(2,128)(2,1)S(1)} %copy.37), channel_id=1, replica_groups=mesh['dp'=64,'tensor'=4] {'tensor'}, dimensions={2} | all-to-all | bytes 2097152 | tf_op jit(solution)/shard_map/all_to_all | solution.py:48
  189.6 0.1 copy.38
  189.8 0.5 copy.39
  190.3 2.1 copy.40
  192.3 9.4 %all-to-all-start.2 = ((bf16[2,1024,256]{2,0,1:T(2,128)(2,1)}), bf16[2,1024,256]{2,0,1:T(2,128)(2,1)S(1)}, u32[]{:S(2)}, u32[]{:S(2)}) async-start(bf16[2,1024,256]{2,0,1:T(2,128)(2,1)} %copy.40), calls=%async_computation.2 | async-start | bytes 2097152 | tf_op jit(solution)/shard_map/all_to_all | solution.py:47
  201.8 0.1 fusion.11
  201.9 77.7 %all-reduce = (f32[48]{0:T(128)S(1)}, f32[48]{0:T(128)S(1)}) all-reduce(f32[48]{0:T(128)S(1)} %get-tuple-element.6, f32[48]{0:T(128)S(1)} %compare_select_fusion.2), channel_id=1, replica_groups=mesh['dp'=64,'tensor'=4] {'dp','tensor'}, use_global_device_ids=true, to_apply=%region_1.0 | all-reduce | flops 96 | bytes 768 | tf_op jit(solution)/shard_map/psum | solution.py:58
  279.6 0.0 copy-start.1
  279.6 0.0 copy-start.2
  279.6 6.0 %bitcast_add_fusion = f32[1,2,256,1024]{3,2,1,0:T(8,128)} fusion(f32[1,2,256,1024]{3,2,1,0:T(8,128)} %param.13, bf16[2,1024,1024]{2,1,0:T(8,128)(2,1)} %bitcast.34, s32[]{:T(128)S(6)} %select_n.19), kind=kOutput, calls=%fused_computation.4 | convolution fusion | flops 1075314688 | bytes 9437188 | tf_op jit(solution)/shard_map/ski,skj->sij/dot_general | solution.py:32
  285.6 0.0 copy-done.1
  285.6 0.0 copy-done.2
  285.6 2.7 bitcast_add_fusion.1
  288.3 0.0 all-to-all-done.2
  288.3 0.1 copy.41
  288.4 0.1 copy.42
  288.5 0.6 gather_fusion
  289.1 0.9 multiply_convert_fusion
  (4 shorter events, 0.0 us)
Async XLA Ops:
  7.2 159.1 %copy-start = (bf16[1,2,256,1024]{3,2,1,0:T(8,128)(2,1)S(1)}, bf16[1,2,256,1024]{3,2,1,0:T(8,128)(2,1)}, u32[]{:S(2)}) copy-start(bf16[1,2,256,1024]{3,2,1,0:T(8,128)(2,1)} %param.14) | copy-start | bytes 3145732
  7.2 3.3 %copy-start.4 = (s32[48]{0:T(128)S(1)}, s32[48]{0:T(128)}, u32[]{:S(2)}) copy-start(s32[48]{0:T(128)} %param.10) | copy-start | bytes 580
  7.2 3.3 %copy-start.5 = (s32[48]{0:T(128)S(1)}, s32[48]{0:T(128)}, u32[]{:S(2)}) copy-start(s32[48]{0:T(128)} %param.11) | copy-start | bytes 580
  7.2 38.0 %all-gather.4.cloned.1.call-start = ((), (), s32[]{:S(2)}) async-start(), calls=%async_computation.3 | async-start | bytes 1966080 | tf_op jit(solution)/shard_map/all_gather | solution.py:22
  45.2 2.5 copy-start.3
  54.3 107.0 %all-to-all-start = ((bf16[128,16,1024]{2,1,0:T(8,128)(2,1)}), bf16[128,16,1024]{2,1,0:T(8,128)(2,1)}, u32[]{:S(2)}, u32[]{:S(2)}) async-start(bf16[128,16,1024]{2,1,0:T(8,128)(2,1)} %scatter_fusion), calls=%async_computation | async-start | bytes 8388608 | tf_op jit(solution)/shard_map/all_to_all | solution.py:28
  66.5 99.7 %all-gather.6.cloned.1.call-start = ((), (), s32[]{:S(2)}) async-start(), calls=%async_computation.4 | async-start | bytes 5242880 | tf_op jit(solution)/shard_map/all_gather | solution.py:41
  192.3 95.9 %all-to-all-start.2 = ((bf16[2,1024,256]{2,0,1:T(2,128)(2,1)}), bf16[2,1024,256]{2,0,1:T(2,128)(2,1)S(1)}, u32[]{:S(2)}, u32[]{:S(2)}) async-start(bf16[2,1024,256]{2,0,1:T(2,128)(2,1)} %copy.40), calls=%async_computation.2 | async-start | bytes 2097152 | tf_op jit(solution)/shard_map/all_to_all | solution.py:47
  279.6 6.0 %copy-start.1 = (bf16[2,64,16,1024]{3,2,1,0:T(8,128)(2,1)S(1)}, bf16[2,64,16,1024]{3,2,1,0:T(8,128)(2,1)}, u32[]{:S(2)}) copy-start(bf16[2,64,16,1024]{3,2,1,0:T(8,128)(2,1)} %copy.34) | copy-start | bytes 12582916
  279.6 6.0 %copy-start.2 = (f32[1,2,256,1024]{3,2,1,0:T(8,128)S(1)}, f32[1,2,256,1024]{3,2,1,0:T(8,128)}, u32[]{:S(2)}) copy-start(f32[1,2,256,1024]{3,2,1,0:T(8,128)} %param.12) | copy-start | bytes 6291460
Sparse Core Ops, SparseCore 0:
  10.6 34.5 all-gather.3
  69.2 51.1 all-gather.5
where the time goes:
time: 297 us
  waiting for transfers between devices  129 us (43%)
  blocking collectives  94 us (32%)
  starting transfers between devices  21.7 us (7%)
  local copies, waits for them, and re-layouts  18.6 us (6%)
  matrix products  14.8 us (5%)
  between operations  14.2 us (5%)
  other arithmetic  4.19 us (1%)
    all_to_all x1, waiting for transfers between devices, per_device(): lax.all_to_all(buffer, 'dp', split_axis=0, concat_axis=1, tiled=True)  94 us
    psum x1, blocking collectives, per_device(): adam_total, root_total = lax.psum((adam_part, root_part), ('dp', 'tensor'))  77.7 us
    all_gather x1, waiting for transfers between devices, per_device(): gathered = lax.all_gather(grad_low, 'tensor', axis=2, tiled=True)  34.7 us
    all_to_all x1, blocking collectives, per_device(): lax.all_to_all(precond, 'tensor', split_axis=2, concat_axis=1, tiled=True)  16.3 us
    all_to_all x1, starting transfers between devices, per_device(): lax.all_to_all(buffer, 'dp', split_axis=0, concat_axis=1, tiled=True)  12.2 us
    all_to_all x1, starting transfers between devices, per_device(): lax.all_to_all(lax.all_to_all(precond, 'tensor', split_axis=2, concat_axi...  9.43 us
    scatter x1, local copies, waits for them, and re-layouts, per_device(): buffer = jnp.zeros((owner_count * slot_count, shard_rows, block_order), j...  6.59 us
    dot_general x1, matrix products, per_device(): jnp.einsum('sik,skj->sij', mixed, lax.all_gather(right_root[0], 'tensor',...  6.14 us
  transfers between devices with their start and end apart: 4, of which 2 were waited for; matrix products, arithmetic and copies ran while one was open for 5% of the time, Pallas kernels for 0%

commit v1 on v0

--- a/solution.py
+++ b/solution.py
@@ -55,7 +55,11 @@
     slot_match = slot_table[:, None] == jnp.arange(slot_count, dtype=jnp.int32)[None, :]
     looked_up = jnp.sum(jnp.where(slot_match, root_slot[None, :], 0.0), axis=1)
     root_part = jnp.where(owner_table == owner_index, looked_up, 0.0)
-    adam_total, root_total = lax.psum((adam_part, root_part), ("dp", "tensor"))
+
+    def match_results(q_in):
+        return jax.lax.psum(jax.lax.psum(q_in, "dp"), "tensor")
+
+    adam_total, root_total = match_results((adam_part, root_part))
     graft_scale = jnp.sqrt(adam_total / (root_total + 1e-06))
     update = (graft_scale[:, None, None] * returned_blocks.astype(jnp.float32)).astype(jnp.bfloat16)
     return (update, new_second, left_new, right_new)

time: 297 us -> 371 us (1.25)
  blocking collectives: 94 us -> 164 us
    psum x1 -> x2, blocking collectives: 77.7 us -> 148 us  [match_results(): return jax.lax.psum(jax.lax.psum(q_in, 'dp'), 'tensor')]
  transfers between devices with their start and end apart: 4 -> 4, of which waited for: 2 -> 2; matrix products, arithmetic and copies ran while one was open for 5% -> 4% of each run, Pallas kernels for 0% -> 0%
where the time goes in v1:
time: 371 us; the launch traced here: 367 us
  blocking collectives  164 us (44%)
  waiting for transfers between devices  129 us (35%)
  starting transfers between devices  21.8 us (6%)
  local copies, waits for them, and re-layouts  18.6 us (5%)
  matrix products  14.8 us (4%)
  between operations  14.2 us (4%)
  other arithmetic  4.19 us (1%)
    psum x2, blocking collectives, match_results(): return jax.lax.psum(jax.lax.psum(q_in, 'dp'), 'tensor')  148 us
    all_to_all x1, waiting for transfers between devices, per_device(): lax.all_to_all(buffer, 'dp', split_axis=0, concat_axis=1, tiled=True)  94 us
    all_gather x1, waiting for transfers between devices, per_device(): gathered = lax.all_gather(grad_low, 'tensor', axis=2, tiled=True)  34.7 us
    all_to_all x1, blocking collectives, per_device(): lax.all_to_all(precond, 'tensor', split_axis=2, concat_axis=1, tiled=True)  16.3 us
    all_to_all x1, starting transfers between devices, per_device(): lax.all_to_all(buffer, 'dp', split_axis=0, concat_axis=1, tiled=True)  12.2 us
    all_to_all x1, starting transfers between devices, per_device(): lax.all_to_all(lax.all_to_all(precond, 'tensor', split_axis=2, concat_axi...  9.43 us
  transfers between devices with their start and end apart: 4, of which 2 were waited for; matrix products, arithmetic and copies ran while one was open for 4% of the time, Pallas kernels for 0%

profile of v1, /device:TPU:1, one launch (start us, length us, event | category | flops | bytes accessed | tf_op | source)
XLA Modules:
  0.0 367.4 jit_solution(11203289321604169583)
XLA Ops:
  7.2 0.0 copy-start
  7.2 0.0 copy-start.4
  7.2 0.0 copy-start.5
  7.2 0.0 all-gather.4.cloned.1.call-start
  7.2 3.2 multiply_reduce_fusion.1
  10.4 0.0 all-gather.4.cloned.1.call-update
  10.5 0.0 copy-done.4
  10.5 0.0 copy-done.5
  10.5 34.7 %all-gather.4.cloned.1.call-done = bf16[48,16,1024]{2,1,0:T(8,128)(2,1)} async-done(((bf16[48,16,256]{2,1,0:T(8,128)(2,1)}), bf16[48,16,1024]{2,1,0:T(8,128)(2,1)}) %all-gather.4.cloned.1.call-update) | async-done | bytes 1572880 | tf_op jit(solution)/shard_map/all_gather | solution.py:22
  45.2 0.0 copy-start.3
  45.2 2.5 broadcast_in_dim.29
  47.7 0.0 copy-done.3
  47.7 6.6 %scatter_fusion = bf16[128,16,1024]{2,1,0:T(8,128)(2,1)} fusion(bf16[128,16,1024]{2,1,0:T(8,128)(2,1)} %broadcast_in_dim.29, s32[48]{0:T(128)S(1)} %compare_select_fusion, bf16[48,16,1024]{2,1,0:T(8,128)(2,1)S(1)} %copy-done.3), kind=kCustom, calls=%fused_computation.1 | custom fusion | bytes 4718784 | tf_op jit(solution)/shard_map/scatter | solution.py:26
  54.3 12.2 %all-to-all-start = ((bf16[128,16,1024]{2,1,0:T(8,128)(2,1)}), bf16[128,16,1024]{2,1,0:T(8,128)(2,1)}, u32[]{:S(2)}, u32[]{:S(2)}) async-start(bf16[128,16,1024]{2,1,0:T(8,128)(2,1)} %scatter_fusion), calls=%async_computation | async-start | bytes 8388608 | tf_op jit(solution)/shard_map/all_to_all | solution.py:28
  66.6 0.0 all-gather.6.cloned.1.call-start
  66.6 0.7 all-gather.6.cloned.1.call-update
  67.3 94.0 %all-to-all-done = bf16[128,16,1024]{2,1,0:T(8,128)(2,1)} async-done(((bf16[128,16,1024]{2,1,0:T(8,128)(2,1)}), bf16[128,16,1024]{2,1,0:T(8,128)(2,1)}, u32[]{:S(2)}, u32[]{:S(2)}) %all-to-all-start) | async-done | bytes 4194336 | tf_op jit(solution)/shard_map/all_to_all | solution.py:28
  161.3 5.0 %copy.34 = bf16[2,64,16,1024]{3,2,1,0:T(8,128)(2,1)} copy(bf16[2,64,16,1024]{3,2,0,1:T(8,128)(2,1)} %bitcast.1) | data formatting | bytes 8388608 | tf_op jit(solution)/shard_map/all_to_all | solution.py:28
  166.2 0.0 all-gather.6.cloned.1.call-done
  166.2 0.0 copy-done
  166.2 6.1 %multiply_reduce_fusion = (f32[2]{0:T(128)S(1)}, bf16[2,256,1024]{2,1,0:T(8,128)(2,1)S(1)}) fusion(bf16[1,2,1024,1024]{3,2,1,0:T(8,128)(2,1)} %all-gather.6.cloned.1.call-done, bf16[2,1024,1024]{2,1,0:T(8,128)(2,1)} %bitcast.33, bf16[1,2,256,1024]{3,2,1,0:T(8,128)(2,1)S(1)} %copy-done), kind=kOutput, calls=%fused_computation.6 | convolution fusion | flops 2150105088 | bytes 10485768 | tf_op jit(solution)/shard_map/sik,skj->sij/dot_general | solution.py:38
  172.4 0.9 copy.37
  173.3 16.3 %all_to_all.54 = bf16[2,256,1024]{1,0,2:T(2,128)(2,1)S(1)} all-to-all(bf16[2,256,1024]{1,0,2:T(2,128)(2,1)S(1)} %copy.37), channel_id=1, replica_groups=mesh['dp'=64,'tensor'=4] {'tensor'}, dimensions={2} | all-to-all | bytes 2097152 | tf_op jit(solution)/shard_map/all_to_all | solution.py:48
  189.6 0.1 copy.38
  189.8 0.5 copy.39
  190.3 2.0 copy.40
  192.4 9.4 %all-to-all-start.2 = ((bf16[2,1024,256]{2,0,1:T(2,128)(2,1)}), bf16[2,1024,256]{2,0,1:T(2,128)(2,1)S(1)}, u32[]{:S(2)}, u32[]{:S(2)}) async-start(bf16[2,1024,256]{2,0,1:T(2,128)(2,1)} %copy.40), calls=%async_computation.2 | async-start | bytes 2097152 | tf_op jit(solution)/shard_map/all_to_all | solution.py:47
  201.8 0.1 fusion.11
  201.9 141.3 %all-reduce = (f32[48]{0:T(128)S(1)}, f32[48]{0:T(128)S(1)}) all-reduce(f32[48]{0:T(128)S(1)} %get-tuple-element.8, f32[48]{0:T(128)S(1)} %compare_select_fusion.2), channel_id=1, replica_groups=mesh['dp'=64,'tensor'=4] {'dp'}, use_global_device_ids=true, to_apply=%region_1.0 | all-reduce | flops 96 | bytes 768 | tf_op jit(solution)/shard_map/psum | solution.py:60
  343.2 6.9 %all-reduce.1 = (f32[48]{0:T(128)S(1)}, f32[48]{0:T(128)S(1)}) all-reduce(f32[48]{0:T(128)S(1)} %get-tuple-element.4, f32[48]{0:T(128)S(1)} %get-tuple-element.5), channel_id=1, replica_groups=mesh['dp'=64,'tensor'=4] {'tensor'}, use_global_device_ids=true, to_apply=%region_2.0 | all-reduce | flops 96 | bytes 768 | tf_op jit(solution)/shard_map/psum | solution.py:60
  350.1 0.0 copy-start.1
  350.1 0.0 copy-start.2
  350.1 6.0 %bitcast_add_fusion = f32[1,2,256,1024]{3,2,1,0:T(8,128)} fusion(f32[1,2,256,1024]{3,2,1,0:T(8,128)} %param.13, bf16[2,1024,1024]{2,1,0:T(8,128)(2,1)} %bitcast.34, s32[]{:T(128)S(6)} %select_n.19), kind=kOutput, calls=%fused_computation.4 | convolution fusion | flops 1075314688 | bytes 9437188 | tf_op jit(solution)/shard_map/ski,skj->sij/dot_general | solution.py:32
  356.1 0.0 copy-done.1
  356.1 0.0 copy-done.2
  356.1 2.7 bitcast_add_fusion.1
  358.8 0.0 all-to-all-done.2
  358.8 0.1 copy.41
  359.0 0.1 copy.42
  359.1 0.6 gather_fusion
  359.7 0.9 multiply_convert_fusion
  (4 shorter events, 0.0 us)
Async XLA Ops:
  7.2 159.1 %copy-start = (bf16[1,2,256,1024]{3,2,1,0:T(8,128)(2,1)S(1)}, bf16[1,2,256,1024]{3,2,1,0:T(8,128)(2,1)}, u32[]{:S(2)}) copy-start(bf16[1,2,256,1024]{3,2,1,0:T(8,128)(2,1)} %param.14) | copy-start | bytes 3145732
  7.2 3.3 copy-start.4
  7.2 3.3 copy-start.5
  7.2 38.0 %all-gather.4.cloned.1.call-start = ((), (), s32[]{:S(2)}) async-start(), calls=%async_computation.3 | async-start | bytes 1966080 | tf_op jit(solution)/shard_map/all_gather | solution.py:22
  45.2 2.5 copy-start.3
  54.3 107.0 %all-to-all-start = ((bf16[128,16,1024]{2,1,0:T(8,128)(2,1)}), bf16[128,16,1024]{2,1,0:T(8,128)(2,1)}, u32[]{:S(2)}, u32[]{:S(2)}) async-start(bf16[128,16,1024]{2,1,0:T(8,128)(2,1)} %scatter_fusion), calls=%async_computation | async-start | bytes 8388608 | tf_op jit(solution)/shard_map/all_to_all | solution.py:28
  66.6 99.7 %all-gather.6.cloned.1.call-start = ((), (), s32[]{:S(2)}) async-start(), calls=%async_computation.4 | async-start | bytes 5242880 | tf_op jit(solution)/shard_map/all_gather | solution.py:41
  192.4 166.4 %all-to-all-start.2 = ((bf16[2,1024,256]{2,0,1:T(2,128)(2,1)}), bf16[2,1024,256]{2,0,1:T(2,128)(2,1)S(1)}, u32[]{:S(2)}, u32[]{:S(2)}) async-start(bf16[2,1024,256]{2,0,1:T(2,128)(2,1)} %copy.40), calls=%async_computation.2 | async-start | bytes 2097152 | tf_op jit(solution)/shard_map/all_to_all | solution.py:47
  350.1 6.0 %copy-start.1 = (bf16[2,64,16,1024]{3,2,1,0:T(8,128)(2,1)S(1)}, bf16[2,64,16,1024]{3,2,1,0:T(8,128)(2,1)}, u32[]{:S(2)}) copy-start(bf16[2,64,16,1024]{3,2,1,0:T(8,128)(2,1)} %copy.34) | copy-start | bytes 12582916
  350.1 6.0 %copy-start.2 = (f32[1,2,256,1024]{3,2,1,0:T(8,128)S(1)}, f32[1,2,256,1024]{3,2,1,0:T(8,128)}, u32[]{:S(2)}) copy-start(f32[1,2,256,1024]{3,2,1,0:T(8,128)} %param.12) | copy-start | bytes 6291460
Sparse Core Ops, SparseCore 0:
  10.6 34.5 all-gather.3
  69.2 51.1 all-gather.5
